TPU v7x, 32 devices: a whole 2x2x4 slice. The times are simulated.
32 devices in a mesh: vec: 8 (over z, core), rep: 4 (over y, x).
Axes of the slice: x: 2, y: 2, z: 4, core: 2. Of those that a mesh axis runs over, the one named last changes fastest.
Arguments:
- vectors: bfloat16 [1024, 1024], P('vec'), may hold values from 0 to 2
- pivot_index: int32 [4, 8], P('rep'), may hold values from 0 to 1023
Outputs:
- similarity: bfloat16 [7, 32, 1024, 128], P(None, 'rep', 'vec')
All inputs are finite; a program needn't handle non-finite values.
Results may differ from a plain program's by a relative error of at most 0.011.
Values may be sent and summed in bfloat16 or wider, within the bound.
A program may use at most 64 MiB of HBM per device.

v0:
```python
import math
import jax
import jax.numpy as jnp
from jax import lax
from jax.sharding import PartitionSpec as P

HALF = 3


def from_behind(block, axis, distance):
    devices = range(lax.axis_size(axis))
    route = [((i - distance) % len(devices), i) for i in devices]
    return lax.ppermute(block, axis, route)


def contract(left, right):
    return lax.dot_general(
        left, right, (((1,), (1,)), ((), ())), preferred_element_type=jnp.float32
    )


def on_device(vectors, pivot_index):
    block_rows, fields = vectors.shape
    position = lax.axis_index("vec")
    wanted = pivot_index.reshape(-1) - position * block_rows
    columns = jnp.arange(block_rows, dtype=jnp.int32)
    onehot = (wanted[:, None] == columns[None, :]).astype(jnp.bfloat16)
    local_rows = jnp.dot(onehot, vectors, preferred_element_type=jnp.float32)
    pivots = lax.psum(local_rows, "vec")
    count = pivots.shape[0]
    centre = jnp.sum(pivots, axis=1) / fields
    scaled = (vectors.astype(jnp.float32)[None, :, :] * pivots[:, None, :]).astype(jnp.bfloat16)
    scaled = scaled.reshape(count * block_rows, fields)
    replicas = lax.axis_size("rep")
    share = block_rows // replicas
    own_rows = lax.dynamic_slice_in_dim(vectors, lax.axis_index("rep") * share, share, 0)
    window = 2 * HALF + 1
    triples = [None] * window
    grams = [None] * window
    triples[HALF] = contract(scaled, vectors)
    grams[HALF] = contract(own_rows, vectors)
    lower = vectors
    upper = vectors
    for reach in range(1, HALF + 1):
        lower = from_behind(lower, "vec", 1)
        upper = from_behind(upper, "vec", -1)
        triples[HALF - reach] = contract(scaled, lower)
        grams[HALF - reach] = contract(own_rows, lower)
        triples[HALF + reach] = contract(scaled, upper)
        grams[HALF + reach] = contract(own_rows, upper)
    triple_all = jnp.stack(triples).reshape(window, count, block_rows, block_rows)
    gram_all = jnp.stack(grams)
    gram_all = lax.all_gather(gram_all, "rep", axis=1, tiled=True)
    similarity = (triple_all - centre[None, :, None, None] * gram_all[:, None, :, :]) / math.sqrt(
        fields
    )
    return similarity.astype(jnp.bfloat16)


def solution(mesh):
    in_specs = (P("vec", None), P("rep", None))
    out_specs = P(None, "rep", "vec", None)
    return jax.shard_map(
        on_device, mesh=mesh, in_specs=in_specs, out_specs=out_specs, check_vma=False
    )
```

profile of v0, /device:TPU:0, one launch (start us, length us, event | category | flops | bytes accessed | tf_op | source)
XLA Modules:
  0.0 71.4 jit_solution(5123657337619987184)
XLA Ops:
  0.0 0.5 collective-permute-start
  0.5 4.0 %collective-permute-start.3 = (bf16[128,1024]{1,0:T(8,128)(2,1)}, bf16[128,1024]{1,0:T(8,128)(2,1)S(1)}, u32[]{:S(2)}, u32[]{:S(2)}) collective-permute-start(bf16[128,1024]{1,0:T(8,128)(2,1)} %param.2), channel_id=1, source_target_pairs={{4,0},{8,4},{12,8},{16,12},{20,16},{24,20},{28,24},{0,28},{5,1},{9... | collective-permute-start | bytes 786440 | tf_op jit(solution)/shard_map/ppermute | solution.py:13
  4.5 4.5 %collective-permute-done = bf16[128,1024]{1,0:T(8,128)(2,1)S(1)} collective-permute-done((bf16[128,1024]{1,0:T(8,128)(2,1)}, bf16[128,1024]{1,0:T(8,128)(2,1)S(1)}, u32[]{:S(2)}, u32[]{:S(2)}) %collective-permute-start) | collective-permute-done | bytes 262176 | tf_op jit(solution)/shard_map/ppermute | solution.py:13
  9.0 0.0 collective-permute-start.1
  9.0 0.7 subtract_bitcast_fusion
  9.7 0.0 collective-permute-done.3
  9.7 3.5 %collective-permute-start.4 = (bf16[128,1024]{1,0:T(8,128)(2,1)S(1)}, bf16[128,1024]{1,0:T(8,128)(2,1)S(1)}, u32[]{:S(2)}, u32[]{:S(2)}) collective-permute-start(bf16[128,1024]{1,0:T(8,128)(2,1)S(1)} %collective-permute-done.3), channel_id=1, source_target_pairs={{4,0},{8,4},{12,8},{16,12},{20,16},{24,20},{28,24},{0,28},{5,1},{9... | collective-permute-start | bytes 786440 | tf_op jit(solution)/shard_map/ppermute | solution.py:13
  13.2 3.5 %collective-permute-done.1 = bf16[128,1024]{1,0:T(8,128)(2,1)S(1)} collective-permute-done((bf16[128,1024]{1,0:T(8,128)(2,1)S(1)}, bf16[128,1024]{1,0:T(8,128)(2,1)S(1)}, u32[]{:S(2)}, u32[]{:S(2)}) %collective-permute-start.1) | collective-permute-done | bytes 262176 | tf_op jit(solution)/shard_map/ppermute | solution.py:13
  16.7 1.1 %fusion.56 = f32[8,1024]{1,0:T(8,128)S(1)} fusion(bf16[128,1024]{1,0:T(8,128)(2,1)} %param.2, s32[8]{0:T(128)S(1)} %subtract_bitcast_fusion), kind=kOutput, calls=%fused_computation.66 | convolution fusion | flops 2098176 | bytes 294944 | tf_op jit(solution)/shard_map/dot_general | solution.py:28
  17.8 1.0 %convert_element_type.21 = f32[128,1024]{1,0:T(8,128)S(1)} convert(bf16[128,1024]{1,0:T(8,128)(2,1)} %param.2) | non-fusion elementwise | flops 131072 | bytes 786432 | tf_op jit(solution)/shard_map/convert_element_type | solution.py:32
  18.8 29.4 %psum.7 = f32[8,1024]{1,0:T(8,128)S(1)} all-reduce(f32[8,1024]{1,0:T(8,128)S(1)} %fusion.56), channel_id=1, replica_groups=mesh['vec'=8,'rep'=4] {'vec'}, use_global_device_ids=true, to_apply=%region_0.0 | all-reduce | flops 8192 | bytes 65536 | tf_op jit(solution)/shard_map/psum | solution.py:29
  48.3 0.1 reduce_sum.9
  48.4 0.0 collective-permute-done.4
  48.4 0.1 collective-permute-start.5
  48.5 0.0 collective-permute-done.2
  48.5 1.0 %fusion.41 = f32[7,32,128]{2,1,0:T(8,128)S(1)} fusion(bf16[128,1024]{1,0:T(8,128)(2,1)S(1)} %collective-permute-done.2, bf16[128,1024]{1,0:T(8,128)(2,1)} %param.2, s32[]{:T(128)S(6)} %select_n.3), kind=kOutput, calls=%fused_computation.50 | convolution fusion | flops 8388607 | bytes 344068 | tf_op jit(solution)/shard_map/dot_general | solution.py:17
  49.5 1.0 %fusion.40 = f32[7,32,128]{2,1,0:T(8,128)S(1)} fusion(f32[7,32,128]{2,1,0:T(8,128)S(1)} %fusion.41, bf16[128,1024]{1,0:T(8,128)(2,1)S(1)} %collective-permute-done.1, bf16[128,1024]{1,0:T(8,128)(2,1)} %param.2, s32[]{:T(128)S(6)} %select_n.3), kind=kOutput, calls=%fused_computation.48 | convolution fusion | flops 8388608 | bytes 344068 | tf_op jit(solution)/shard_map/dot_general | solution.py:17
  50.5 1.0 %fusion.39 = f32[7,32,128]{2,1,0:T(8,128)S(1)} fusion(f32[7,32,128]{2,1,0:T(8,128)S(1)} %fusion.40, bf16[128,1024]{1,0:T(8,128)(2,1)S(1)} %collective-permute-done, bf16[128,1024]{1,0:T(8,128)(2,1)} %param.2, s32[]{:T(128)S(6)} %select_n.3), kind=kOutput, calls=%fused_computation.46 | convolution fusion | flops 8388608 | bytes 344068 | tf_op jit(solution)/shard_map/dot_general | solution.py:17
  51.6 1.2 %fusion.38 = f32[7,32,128]{2,1,0:T(8,128)S(1)} fusion(f32[7,32,128]{2,1,0:T(8,128)S(1)} %fusion.39, bf16[128,1024]{1,0:T(8,128)(2,1)} %param.2, s32[]{:T(128)S(6)} %select_n.3), kind=kOutput, calls=%fused_computation.44 | convolution fusion | flops 8388608 | bytes 344068 | tf_op jit(solution)/shard_map/dot_general | solution.py:17
  52.8 0.7 %fusion.22 = f32[7,8,128,128]{3,2,1,0:T(8,128)S(1)} fusion(f32[8,1024]{1,0:T(8,128)S(1)} %psum.7, f32[128,1024]{1,0:T(8,128)S(1)} %convert_element_type.21, bf16[128,1024]{1,0:T(8,128)(2,1)S(1)} %collective-permute-done.2), kind=kOutput, calls=%fused_computation.24 | convolution fusion | flops 270532608 | bytes 1343488 | tf_op jit(solution)/shard_map/dot_general | solution.py:17
  53.6 0.7 fusion.24
  54.3 0.7 fusion.26
  55.0 0.2 fusion.37
  55.2 0.2 fusion.36
  55.4 0.7 %fusion.28 = f32[7,8,128,128]{3,2,1,0:T(8,128)S(1)} fusion(f32[7,8,128,128]{3,2,1,0:T(8,128)S(1)} %fusion.26, f32[8,1024]{1,0:T(8,128)S(1)} %psum.7, f32[128,1024]{1,0:T(8,128)S(1)} %convert_element_type.21, bf16[128,1024]{1,0:T(8,128)(2,1)S(1)} %copy-done), kind=kOutput, calls=%fused_computation.30 | convolution fusion | flops 270532608 | bytes 1343488 | tf_op jit(solution)/shard_map/dot_general | solution.py:17
  56.1 0.0 collective-permute-done.5
  56.1 0.2 fusion.35
  56.3 11.0 %all_gather.3 = f32[7,128,128]{2,1,0:T(8,128)S(1)} all-gather(f32[7,32,128]{2,1,0:T(8,128)S(1)} %fusion.35), channel_id=1, replica_groups=mesh['vec'=8,'rep'=4] {'rep'}, dimensions={1}, use_global_device_ids=true | all-gather | bytes 573440 | tf_op jit(solution)/shard_map/all_gather | solution.py:53
  67.3 0.7 fusion.30
  68.0 0.7 fusion.32
  68.8 0.7 fusion.34
  69.5 1.9 %multiply_convert_fusion.8 = bf16[7,8,128,128]{3,2,1,0:T(8,128)(2,1)} fusion(f32[7,8,128,128]{3,2,1,0:T(8,128)S(1)} %fusion.34, f32[7,128,128]{2,1,0:T(8,128)S(1)} %all_gather.3, f32[8]{0:T(128)S(1)} %broadcast_multiply_fusion), kind=kLoop, calls=%fused_computation.8 | loop fusion | flops 3670016 | bytes 5963808 | tf_op jit(solution)/shard_map/convert_element_type | solution.py:57
  (4 shorter events, 0.0 us)
Async XLA Ops:
  0.0 9.0 %collective-permute-start = (bf16[128,1024]{1,0:T(8,128)(2,1)}, bf16[128,1024]{1,0:T(8,128)(2,1)S(1)}, u32[]{:S(2)}, u32[]{:S(2)}) collective-permute-start(bf16[128,1024]{1,0:T(8,128)(2,1)} %param.2), channel_id=1, source_target_pairs={{28,0},{0,4},{4,8},{8,12},{12,16},{16,20},{20,24},{24,28},{29,1},{... | collective-permute-start | bytes 786440 | tf_op jit(solution)/shard_map/ppermute | solution.py:13
  0.5 9.2 %collective-permute-start.3 = (bf16[128,1024]{1,0:T(8,128)(2,1)}, bf16[128,1024]{1,0:T(8,128)(2,1)S(1)}, u32[]{:S(2)}, u32[]{:S(2)}) collective-permute-start(bf16[128,1024]{1,0:T(8,128)(2,1)} %param.2), channel_id=1, source_target_pairs={{4,0},{8,4},{12,8},{16,12},{20,16},{24,20},{28,24},{0,28},{5,1},{9... | collective-permute-start | bytes 786440 | tf_op jit(solution)/shard_map/ppermute | solution.py:13
  9.0 7.7 %collective-permute-start.1 = (bf16[128,1024]{1,0:T(8,128)(2,1)S(1)}, bf16[128,1024]{1,0:T(8,128)(2,1)S(1)}, u32[]{:S(2)}, u32[]{:S(2)}) collective-permute-start(bf16[128,1024]{1,0:T(8,128)(2,1)S(1)} %collective-permute-done), channel_id=1, source_target_pairs={{28,0},{0,4},{4,8},{8,12},{12,16},{16,20},{20,24},{24,28},{29,1},{... | collective-permute-start | bytes 786440 | tf_op jit(solution)/shard_map/ppermute | solution.py:13
  9.7 38.7 %collective-permute-start.4 = (bf16[128,1024]{1,0:T(8,128)(2,1)S(1)}, bf16[128,1024]{1,0:T(8,128)(2,1)S(1)}, u32[]{:S(2)}, u32[]{:S(2)}) collective-permute-start(bf16[128,1024]{1,0:T(8,128)(2,1)S(1)} %collective-permute-done.3), channel_id=1, source_target_pairs={{4,0},{8,4},{12,8},{16,12},{20,16},{24,20},{28,24},{0,28},{5,1},{9... | collective-permute-start | bytes 786440 | tf_op jit(solution)/shard_map/ppermute | solution.py:13
  16.7 31.8 %collective-permute-start.2 = (bf16[128,1024]{1,0:T(8,128)(2,1)S(1)}, bf16[128,1024]{1,0:T(8,128)(2,1)S(1)}, u32[]{:S(2)}, u32[]{:S(2)}) collective-permute-start(bf16[128,1024]{1,0:T(8,128)(2,1)S(1)} %collective-permute-done.1), channel_id=1, source_target_pairs={{28,0},{0,4},{4,8},{8,12},{12,16},{16,20},{20,24},{24,28},{29,1},{... | collective-permute-start | bytes 786440 | tf_op jit(solution)/shard_map/ppermute | solution.py:13
  48.4 7.7 %collective-permute-start.5 = (bf16[128,1024]{1,0:T(8,128)(2,1)S(1)}, bf16[128,1024]{1,0:T(8,128)(2,1)S(1)}, u32[]{:S(2)}, u32[]{:S(2)}) collective-permute-start(bf16[128,1024]{1,0:T(8,128)(2,1)S(1)} %collective-permute-done.4), channel_id=1, source_target_pairs={{4,0},{8,4},{12,8},{16,12},{20,16},{24,20},{28,24},{0,28},{5,1},{9... | collective-permute-start | bytes 786440 | tf_op jit(solution)/shard_map/ppermute | solution.py:13
  52.8 2.2 %copy-start = (bf16[128,1024]{1,0:T(8,128)(2,1)S(1)}, bf16[128,1024]{1,0:T(8,128)(2,1)}, u32[]{:S(2)}) copy-start(bf16[128,1024]{1,0:T(8,128)(2,1)} %param.2) | copy-start | bytes 786436
where the time goes:
time: 71.7 us; the launch traced here: 71.4 us
  blocking collectives  40.5 us (56%)
  matrix products  11 us (15%)
  starting transfers between devices  8.13 us (11%)
  waiting for transfers between devices  7.96 us (11%)
  other arithmetic  3.69 us (5%)
    psum x1, blocking collectives, on_device(): pivots = lax.psum(local_rows, 'vec')  29.4 us
    all_gather x1, blocking collectives, on_device(): gram_all = lax.all_gather(gram_all, 'rep', axis=1, tiled=True)  11 us
    dot_general x14, matrix products, contract(): lax.dot_general(left, right, (((1,), (1,)), ((), ())), preferred_element_...  9.87 us
    ppermute x6, starting transfers between devices, from_behind(): return lax.ppermute(block, axis, route)  8.13 us
    ppermute x6, waiting for transfers between devices, from_behind(): return lax.ppermute(block, axis, route)  7.96 us
    convert_element_type x1, other arithmetic, on_device(): return similarity.astype(jnp.bfloat16)  1.9 us
  transfers between devices with their start and end apart: 6, of which 2 were waited for; matrix products, arithmetic and copies ran while one was open for 15% of the time, Pallas kernels for 0%

commit v1 on v0

--- a/solution.py
+++ b/solution.py
@@ -50,7 +50,9 @@
         grams[HALF + reach] = contract(own_rows, upper)
     triple_all = jnp.stack(triples).reshape(window, count, block_rows, block_rows)
     gram_all = jnp.stack(grams)
-    gram_all = lax.all_gather(gram_all, "rep", axis=1, tiled=True)
+    gram_all = jnp.concatenate(
+        jax.lax.all_to_all(jnp.stack([gram_all] * jax.lax.axis_size("rep")), "rep", 0, 0), axis=1
+    )
     similarity = (triple_all - centre[None, :, None, None] * gram_all[:, None, :, :]) / math.sqrt(
         fields
     )

time: 71.7 us -> 75.8 us (1.057)
  blocking collectives: 40.5 us -> 29.4 us
  starting transfers between devices: 8.13 us -> 12.8 us
  waiting for transfers between devices: 7.96 us -> 11.4 us
  local copies, waits for them, and re-layouts: 0.01 us -> 2.45 us
  matrix products: 11 us -> 13.4 us
  other arithmetic: 3.69 us -> 5.72 us
    all_gather x1 -> x0, blocking collectives: 11 us -> none  [on_device(): gram_all = lax.all_gather(gram_all, 'rep', axis=1, tiled=True)]
    all_to_all x0 -> x1, starting transfers between devices: none -> 4.67 us  [on_device(): jax.lax.all_to_all(jnp.stack([gram_all] * jax.lax.axis_size('rep')), 'rep...]
    all_to_all x0 -> x1, waiting for transfers between devices: none -> 3.45 us  [on_device(): jax.lax.all_to_all(jnp.stack([gram_all] * jax.lax.axis_size('rep')), 'rep...]
    dot_general x14, matrix products: 9.87 us -> 12.3 us  [contract(): lax.dot_general(left, right, (((1,), (1,)), ((), ())), preferred_element_...]
    convert_element_type x1, other arithmetic: 1.9 us -> 3.93 us  [on_device(): return similarity.astype(jnp.bfloat16)]
    unnamed x2 -> x4, local copies, waits for them, and re-layouts: 0.01 us -> 1.6 us
    another operation x0 -> x1, local copies, waits for them, and re-layouts: none -> 0.82 us  [on_device(): jnp.stack([gram_all] * jax.lax.axis_size('rep'))]
  transfers between devices with their start and end apart: 6 -> 7, of which waited for: 2 -> 3; matrix products, arithmetic and copies ran while one was open for 15% -> 20% of each run, Pallas kernels for 0% -> 0%
where the time goes in v1:
time: 75.8 us; the launch traced here: 75.3 us
  blocking collectives  29.4 us (39%)
  matrix products  13.4 us (18%)
  starting transfers between devices  12.8 us (17%)
  waiting for transfers between devices  11.4 us (15%)
  other arithmetic  5.72 us (8%)
  local copies, waits for them, and re-layouts  2.45 us (3%)
    psum x1, blocking collectives, on_device(): pivots = lax.psum(local_rows, 'vec')  29.4 us
    dot_general x14, matrix products, contract(): lax.dot_general(left, right, (((1,), (1,)), ((), ())), preferred_element_...  12.3 us
    ppermute x6, starting transfers between devices, from_behind(): return lax.ppermute(block, axis, route)  8.13 us
    ppermute x6, waiting for transfers between devices, from_behind(): return lax.ppermute(block, axis, route)  7.96 us
    all_to_all x1, starting transfers between devices, on_device(): jax.lax.all_to_all(jnp.stack([gram_all] * jax.lax.axis_size('rep')), 'rep...  4.67 us
    convert_element_type x1, other arithmetic, on_device(): return similarity.astype(jnp.bfloat16)  3.93 us
    all_to_all x1, waiting for transfers between devices, on_device(): jax.lax.all_to_all(jnp.stack([gram_all] * jax.lax.axis_size('rep')), 'rep...  3.45 us
    unnamed x4, local copies, waits for them, and re-layouts  1.6 us
  transfers between devices with their start and end apart: 7, of which 3 were waited for; matrix products, arithmetic and copies ran while one was open for 20% of the time, Pallas kernels for 0%

profile of v1, /device:TPU:0, one launch (start us, length us, event | category | flops | bytes accessed | tf_op | source)
XLA Modules:
  0.0 75.3 jit_solution(11866600567068199172)
XLA Ops:
  0.0 0.5 collective-permute-start
  0.5 4.0 %collective-permute-start.3 = (bf16[128,1024]{1,0:T(8,128)(2,1)}, bf16[128,1024]{1,0:T(8,128)(2,1)S(1)}, u32[]{:S(2)}, u32[]{:S(2)}) collective-permute-start(bf16[128,1024]{1,0:T(8,128)(2,1)} %param.2), channel_id=1, source_target_pairs={{4,0},{8,4},{12,8},{16,12},{20,16},{24,20},{28,24},{0,28},{5,1},{9... | collective-permute-start | bytes 786440 | tf_op jit(solution)/shard_map/ppermute | solution.py:13
  4.5 4.5 %collective-permute-done = bf16[128,1024]{1,0:T(8,128)(2,1)S(1)} collective-permute-done((bf16[128,1024]{1,0:T(8,128)(2,1)}, bf16[128,1024]{1,0:T(8,128)(2,1)S(1)}, u32[]{:S(2)}, u32[]{:S(2)}) %collective-permute-start) | collective-permute-done | bytes 262176 | tf_op jit(solution)/shard_map/ppermute | solution.py:13
  9.0 0.7 subtract_bitcast_fusion
  9.7 0.0 collective-permute-done.3
  9.7 3.5 %collective-permute-start.4 = (bf16[128,1024]{1,0:T(8,128)(2,1)S(1)}, bf16[128,1024]{1,0:T(8,128)(2,1)S(1)}, u32[]{:S(2)}, u32[]{:S(2)}) collective-permute-start(bf16[128,1024]{1,0:T(8,128)(2,1)S(1)} %collective-permute-done.3), channel_id=1, source_target_pairs={{4,0},{8,4},{12,8},{16,12},{20,16},{24,20},{28,24},{0,28},{5,1},{9... | collective-permute-start | bytes 786440 | tf_op jit(solution)/shard_map/ppermute | solution.py:13
  13.2 3.5 %collective-permute-done.1 = bf16[128,1024]{1,0:T(8,128)(2,1)S(1)} collective-permute-done((bf16[128,1024]{1,0:T(8,128)(2,1)S(1)}, bf16[128,1024]{1,0:T(8,128)(2,1)S(1)}, u32[]{:S(2)}, u32[]{:S(2)}) %collective-permute-start.1) | collective-permute-done | bytes 262176 | tf_op jit(solution)/shard_map/ppermute | solution.py:13
  16.7 1.1 %fusion.56 = f32[8,1024]{1,0:T(8,128)S(1)} fusion(bf16[128,1024]{1,0:T(8,128)(2,1)} %param.2, s32[8]{0:T(128)S(1)} %subtract_bitcast_fusion), kind=kOutput, calls=%fused_computation.66 | convolution fusion | flops 2098176 | bytes 294944 | tf_op jit(solution)/shard_map/dot_general | solution.py:28
  17.8 1.0 %convert_element_type.21 = f32[128,1024]{1,0:T(8,128)S(1)} convert(bf16[128,1024]{1,0:T(8,128)(2,1)} %param.2) | non-fusion elementwise | flops 131072 | bytes 786432 | tf_op jit(solution)/shard_map/convert_element_type | solution.py:32
  18.8 29.4 %psum.7 = f32[8,1024]{1,0:T(8,128)S(1)} all-reduce(f32[8,1024]{1,0:T(8,128)S(1)} %fusion.56), channel_id=1, replica_groups=mesh['vec'=8,'rep'=4] {'vec'}, use_global_device_ids=true, to_apply=%region_0.0 | all-reduce | flops 8192 | bytes 65536 | tf_op jit(solution)/shard_map/psum | solution.py:29
  48.3 0.1 reduce_sum.9
  48.4 0.0 collective-permute-done.4
  48.4 0.1 collective-permute-start.5
  48.5 1.0 %fusion.41 = f32[7,32,128]{2,1,0:T(8,128)S(1)} fusion(bf16[128,1024]{1,0:T(8,128)(2,1)S(1)} %collective-permute-done.2, bf16[128,1024]{1,0:T(8,128)(2,1)} %param.2, s32[]{:T(128)S(6)} %select_n.3), kind=kOutput, calls=%fused_computation.50 | convolution fusion | flops 8388607 | bytes 344068 | tf_op jit(solution)/shard_map/dot_general | solution.py:17
  49.5 1.0 %fusion.40 = f32[7,32,128]{2,1,0:T(8,128)S(1)} fusion(f32[7,32,128]{2,1,0:T(8,128)S(1)} %fusion.41, bf16[128,1024]{1,0:T(8,128)(2,1)S(1)} %collective-permute-done.1, bf16[128,1024]{1,0:T(8,128)(2,1)} %param.2, s32[]{:T(128)S(6)} %select_n.3), kind=kOutput, calls=%fused_computation.48 | convolution fusion | flops 8388608 | bytes 344068 | tf_op jit(solution)/shard_map/dot_general | solution.py:17
  50.5 1.0 %fusion.39 = f32[7,32,128]{2,1,0:T(8,128)S(1)} fusion(f32[7,32,128]{2,1,0:T(8,128)S(1)} %fusion.40, bf16[128,1024]{1,0:T(8,128)(2,1)S(1)} %collective-permute-done, bf16[128,1024]{1,0:T(8,128)(2,1)} %param.2, s32[]{:T(128)S(6)} %select_n.3), kind=kOutput, calls=%fused_computation.46 | convolution fusion | flops 8388608 | bytes 344068 | tf_op jit(solution)/shard_map/dot_general | solution.py:17
  51.6 1.2 %fusion.38 = f32[7,32,128]{2,1,0:T(8,128)S(1)} fusion(f32[7,32,128]{2,1,0:T(8,128)S(1)} %fusion.39, bf16[128,1024]{1,0:T(8,128)(2,1)} %param.2, s32[]{:T(128)S(6)} %select_n.3), kind=kOutput, calls=%fused_computation.44 | convolution fusion | flops 8388608 | bytes 344068 | tf_op jit(solution)/shard_map/dot_general | solution.py:17
  52.8 0.7 fusion.22
  53.6 0.7 fusion.24
  54.3 0.7 fusion.26
  55.0 0.2 fusion.37
  55.2 0.2 fusion.36
  55.4 0.7 fusion.28
  56.1 0.2 fusion.35
  56.3 1.6 %copy-done.1 = f32[7,8,128,128]{3,2,1,0:T(8,128)} copy-done((f32[7,8,128,128]{3,2,1,0:T(8,128)}, f32[7,8,128,128]{3,2,1,0:T(8,128)S(1)}, u32[]{:S(2)}) %copy-start.1) | copy-done | bytes 3670040
  57.9 0.8 %stack.50 = f32[4,7,32,128]{3,2,1,0:T(8,128)} broadcast(f32[7,32,128]{2,1,0:T(8,128)S(1)} %fusion.35), dimensions={1,2,3} | broadcast | bytes 573440 | tf_op jit(solution)/shard_map/stack | solution.py:54
  58.7 4.7 %all-to-all-start = ((f32[4,7,32,128]{3,2,1,0:T(8,128)}), f32[4,7,32,128]{3,2,1,0:T(8,128)S(1)}, u32[]{:S(2)}, u32[]{:S(2)}) async-start(f32[4,7,32,128]{3,2,1,0:T(8,128)} %stack.50), calls=%async_computation | async-start | bytes 917504 | tf_op jit(solution)/shard_map/all_to_all | solution.py:54
  63.4 1.5 %fusion.30 = f32[7,8,128,128]{3,2,1,0:T(8,128)} fusion(f32[7,8,128,128]{3,2,1,0:T(8,128)} %copy-done.1, f32[8,1024]{1,0:T(8,128)S(1)} %psum.7, f32[128,1024]{1,0:T(8,128)S(1)} %convert_element_type.21, bf16[128,1024]{1,0:T(8,128)(2,1)S(1)} %collective-permute-done.3), kind=kOutput, calls=%fused_computation.32 | convolution fusion | flops 270532608 | bytes 1343488 | tf_op jit(solution)/shard_map/dot_general | solution.py:17
  64.9 1.5 %fusion.32 = f32[7,8,128,128]{3,2,1,0:T(8,128)} fusion(f32[7,8,128,128]{3,2,1,0:T(8,128)} %fusion.30, f32[8,1024]{1,0:T(8,128)S(1)} %psum.7, f32[128,1024]{1,0:T(8,128)S(1)} %convert_element_type.21, bf16[128,1024]{1,0:T(8,128)(2,1)S(1)} %collective-permute-done.4), kind=kOutput, calls=%fused_computation.34 | convolution fusion | flops 270532608 | bytes 1343488 | tf_op jit(solution)/shard_map/dot_general | solution.py:17
  66.4 1.5 %fusion.34 = f32[7,8,128,128]{3,2,1,0:T(8,128)} fusion(f32[7,8,128,128]{3,2,1,0:T(8,128)} %fusion.32, f32[8,1024]{1,0:T(8,128)S(1)} %psum.7, f32[128,1024]{1,0:T(8,128)S(1)} %convert_element_type.21, bf16[128,1024]{1,0:T(8,128)(2,1)S(1)} %collective-permute-done.5), kind=kOutput, calls=%fused_computation.36 | convolution fusion | flops 270532608 | bytes 1343488 | tf_op jit(solution)/shard_map/dot_general | solution.py:17
  67.9 3.4 %all-to-all-done = f32[4,7,32,128]{3,2,1,0:T(8,128)S(1)} async-done(((f32[4,7,32,128]{3,2,1,0:T(8,128)}), f32[4,7,32,128]{3,2,1,0:T(8,128)S(1)}, u32[]{:S(2)}, u32[]{:S(2)}) %all-to-all-start) | async-done | bytes 458784 | tf_op jit(solution)/shard_map/all_to_all | solution.py:54
  71.4 3.9 %multiply_convert_fusion.8 = bf16[7,8,128,128]{3,2,1,0:T(8,128)(2,1)} fusion(f32[7,8,128,128]{3,2,1,0:T(8,128)} %fusion.34, f32[7,128,128]{2,1,0:T(8,128)S(1)} %bitcast.90, f32[8]{0:T(128)S(1)} %broadcast_multiply_fusion), kind=kLoop, calls=%fused_computation.8 | loop fusion | flops 3670016 | bytes 5963808 | tf_op jit(solution)/shard_map/convert_element_type | solution.py:59
  (9 shorter events, 0.1 us)
Async XLA Ops:
  0.0 9.0 %collective-permute-start = (bf16[128,1024]{1,0:T(8,128)(2,1)}, bf16[128,1024]{1,0:T(8,128)(2,1)S(1)}, u32[]{:S(2)}, u32[]{:S(2)}) collective-permute-start(bf16[128,1024]{1,0:T(8,128)(2,1)} %param.2), channel_id=1, source_target_pairs={{28,0},{0,4},{4,8},{8,12},{12,16},{16,20},{20,24},{24,28},{29,1},{... | collective-permute-start | bytes 786440 | tf_op jit(solution)/shard_map/ppermute | solution.py:13
  0.5 9.2 %collective-permute-start.3 = (bf16[128,1024]{1,0:T(8,128)(2,1)}, bf16[128,1024]{1,0:T(8,128)(2,1)S(1)}, u32[]{:S(2)}, u32[]{:S(2)}) collective-permute-start(bf16[128,1024]{1,0:T(8,128)(2,1)} %param.2), channel_id=1, source_target_pairs={{4,0},{8,4},{12,8},{16,12},{20,16},{24,20},{28,24},{0,28},{5,1},{9... | collective-permute-start | bytes 786440 | tf_op jit(solution)/shard_map/ppermute | solution.py:13
  9.0 7.7 %collective-permute-start.1 = (bf16[128,1024]{1,0:T(8,128)(2,1)S(1)}, bf16[128,1024]{1,0:T(8,128)(2,1)S(1)}, u32[]{:S(2)}, u32[]{:S(2)}) collective-permute-start(bf16[128,1024]{1,0:T(8,128)(2,1)S(1)} %collective-permute-done), channel_id=1, source_target_pairs={{28,0},{0,4},{4,8},{8,12},{12,16},{16,20},{20,24},{24,28},{29,1},{... | collective-permute-start | bytes 786440 | tf_op jit(solution)/shard_map/ppermute | solution.py:13
  9.7 38.7 %collective-permute-start.4 = (bf16[128,1024]{1,0:T(8,128)(2,1)S(1)}, bf16[128,1024]{1,0:T(8,128)(2,1)S(1)}, u32[]{:S(2)}, u32[]{:S(2)}) collective-permute-start(bf16[128,1024]{1,0:T(8,128)(2,1)S(1)} %collective-permute-done.3), channel_id=1, source_target_pairs={{4,0},{8,4},{12,8},{16,12},{20,16},{24,20},{28,24},{0,28},{5,1},{9... | collective-permute-start | bytes 786440 | tf_op jit(solution)/shard_map/ppermute | solution.py:13
  16.7 31.8 %collective-permute-start.2 = (bf16[128,1024]{1,0:T(8,128)(2,1)S(1)}, bf16[128,1024]{1,0:T(8,128)(2,1)S(1)}, u32[]{:S(2)}, u32[]{:S(2)}) collective-permute-start(bf16[128,1024]{1,0:T(8,128)(2,1)S(1)} %collective-permute-done.1), channel_id=1, source_target_pairs={{28,0},{0,4},{4,8},{8,12},{12,16},{16,20},{20,24},{24,28},{29,1},{... | collective-permute-start | bytes 786440 | tf_op jit(solution)/shard_map/ppermute | solution.py:13
  48.4 7.7 %collective-permute-start.5 = (bf16[128,1024]{1,0:T(8,128)(2,1)S(1)}, bf16[128,1024]{1,0:T(8,128)(2,1)S(1)}, u32[]{:S(2)}, u32[]{:S(2)}) collective-permute-start(bf16[128,1024]{1,0:T(8,128)(2,1)S(1)} %collective-permute-done.4), channel_id=1, source_target_pairs={{4,0},{8,4},{12,8},{16,12},{20,16},{24,20},{28,24},{0,28},{5,1},{9... | collective-permute-start | bytes 786440 | tf_op jit(solution)/shard_map/ppermute | solution.py:13
  52.8 2.2 %copy-start = (bf16[128,1024]{1,0:T(8,128)(2,1)S(1)}, bf16[128,1024]{1,0:T(8,128)(2,1)}, u32[]{:S(2)}) copy-start(bf16[128,1024]{1,0:T(8,128)(2,1)} %param.2) | copy-start | bytes 786436
  56.1 1.8 %copy-start.1 = (f32[7,8,128,128]{3,2,1,0:T(8,128)}, f32[7,8,128,128]{3,2,1,0:T(8,128)S(1)}, u32[]{:S(2)}) copy-start(f32[7,8,128,128]{3,2,1,0:T(8,128)S(1)} %fusion.28) | copy-start | bytes 11010052
  58.7 12.6 %all-to-all-start = ((f32[4,7,32,128]{3,2,1,0:T(8,128)}), f32[4,7,32,128]{3,2,1,0:T(8,128)S(1)}, u32[]{:S(2)}, u32[]{:S(2)}) async-start(f32[4,7,32,128]{3,2,1,0:T(8,128)} %stack.50), calls=%async_computation | async-start | bytes 917504 | tf_op jit(solution)/shard_map/all_to_all | solution.py:54
